TPU v7x, 128 devices: a whole 4x4x4 slice. The times are simulated.
128 devices in a mesh: rack: 64 (over y, z, x_hi, core), queue: 2 (over x_lo).
Axes of the slice: x: 4 (x_hi: 2, x_lo: 2; x = x_hi * 2 + x_lo), y: 4, z: 4, core: 2. Of those that a mesh axis runs over, the one named last changes fastest.
Arguments:
- state: float32 [4096, 4096], P('rack', 'queue'), may hold values from -6 to 6
- queue_blocks: float32 [16, 3, 256, 256], P('queue'), may hold values from -0.21875 to 0.21875
- queue_rows: int32 [16, 3], P('queue'), may hold values from 0 to 15, as said below
- kill_blocks: float32 [16, 3, 256, 256], P('queue'), may hold values from -0.21875 to 0.21875
- kill_rows: int32 [16, 3], P('queue'), may hold values from 0 to 15, as said below
- rate_index: int32 [12], replicated, may hold values from 0 to 7
- rate_table: float32 [8, 2], replicated, may hold values from 0.1 to 2
Outputs:
- advanced: float32 [4096, 4096], P('rack', 'queue')
Inputs may be any that keep to these rules, and one draw needn't show every extreme that they name: `queue_rows`: column block c's first row block is c, and its three row blocks are distinct. `kill_rows`: column block c's first row block is c, and its three row blocks are distinct.
All inputs are finite; a program needn't handle non-finite values.
Results may differ from a plain program's by a relative error of at most 0.0001.
Values sent between devices are 32-bit elements; how exact they have to be, the bound alone decides.
A program may use at most 128 MiB of HBM per device.

v0:
```python
import jax
import jax.numpy as jnp
from jax import lax
from jax.sharding import PartitionSpec as P

STEPS = 2


def from_partner(value, axis, stride):
    mask = 2**stride
    pairs = [(source, source ^ mask) for source in range(lax.axis_size(axis))]
    return lax.ppermute(value, axis, pairs)


def apply_blocks(whole, blocks, rows):
    patterns = whole.shape[0]
    pieces = whole.reshape(patterns, -1, blocks.shape[2])
    chosen = jnp.take(pieces, rows, axis=1)
    result = jnp.einsum(
        "pcjt,cjts->pcs",
        chosen,
        blocks,
        precision=lax.Precision.HIGHEST,
        preferred_element_type=jnp.float32,
    )
    return result.reshape(patterns, -1)


def bit_terms(current, killed, fail, repair, first, count):
    total = jnp.zeros_like(current)
    rows = current.shape[0]
    for bit in range(count):
        shape = (rows // 2 ** (bit + 1), 2, 2**bit) + current.shape[1:]
        upper = current.reshape(shape)
        lower = killed.reshape(shape)
        term = jnp.stack(
            (repair[first + bit] * upper[:, 1], fail[first + bit] * lower[:, 0]), axis=1
        )
        total = total + term.reshape(current.shape)
    return total


def local(state, queue_blocks, queue_rows, kill_blocks, kill_rows, rate_index, rate_table):
    fail = rate_table[rate_index, 0]
    repair = rate_table[rate_index, 1]
    scale_sum = 1.0 + jnp.sum(fail + repair)
    patterns = state.shape[0]
    low_count = patterns.bit_length() - 1
    high_count = lax.axis_size("rack").bit_length() - 1
    rack_place = lax.axis_index("rack")
    pattern = lax.broadcasted_iota(jnp.int32, (patterns, 1), 0)
    leaving = jnp.zeros((patterns, 1), jnp.float32)
    for bit in range(low_count):
        flag = pattern // 2**bit % 2
        leaving = leaving + jnp.where(flag == 1, repair[bit], fail[bit])
    for bit in range(high_count):
        flag = rack_place // 2**bit % 2
        leaving = leaving + jnp.where(flag == 1, repair[low_count + bit], fail[low_count + bit])
    current = state
    for step in range(STEPS):
        whole = lax.all_gather(current, "queue", axis=1, tiled=True)
        queue_part = apply_blocks(whole, queue_blocks, queue_rows)
        killed = apply_blocks(whole, kill_blocks, kill_rows)
        rack_part = bit_terms(current, killed, fail, repair, 0, low_count)
        order = range(high_count)
        for bit in order:
            flag = rack_place // 2**bit % 2
            outgoing = jnp.where(flag == 1, current, killed)
            incoming = from_partner(outgoing, "rack", bit)
            rack_part = (
                rack_part
                + jnp.where(flag == 1, fail[low_count + bit], repair[low_count + bit]) * incoming
            )
        current = current + (queue_part + rack_part - leaving * current) / scale_sum
    return current


def solution(mesh):
    placed = (
        P("rack", "queue"),
        P("queue", None, None, None),
        P("queue", None),
        P("queue", None, None, None),
        P("queue", None),
        P(),
        P(),
    )
    return jax.shard_map(
        local, mesh=mesh, in_specs=placed, out_specs=P("rack", "queue"), check_vma=False
    )
```

profile of v0, /device:TPU:0, one launch (start us, length us, event | category | flops | bytes accessed | tf_op | source)
XLA Modules:
  0.0 198.4 jit_solution(13551869775011367674)
XLA Ops:
  10.1 1.2 reshape.448
  15.0 1.3 slice_multiply_fusion.13
  16.4 1.3 slice_multiply_fusion.15
  18.4 1.3 slice_multiply_fusion.19
  27.2 7.4 %add_add_fusion = f32[64]{0:T(128)S(1)} fusion(f32[]{:T(128)S(6)} %select_n.398, f32[]{:T(128)S(6)} %select_n.397, f32[]{:T(128)S(6)} %select_n.396, f32[]{:T(128)S(6)} %select_n.395, f32[]{:T(128)S(6)} %select_n.394, f32[]{:T(128)S(6)} %select_n.393, f32[]{:T(128)} %bitcast.27, f32[]{:T(128)} %bitcast.25, f32[]{:T(128)} %bitcast.23, f32[]{:T(128)} %bitcast.21, ...), kind=kLoop, calls=%fused_computation.162 | loop fusion | flops 7296 | bytes 328 | tf_op jit(solution)/shard_map/add | solution.py:58
  43.7 1.5 slice_multiply_fusion.21
  45.2 1.6 slice_multiply_fusion.23
  46.8 1.3 copy.85
  48.1 1.8 gather_fusion.3
  49.9 7.3 %fusion.4 = f32[8,64,256,1]{2,1,3,0:T(8,128)S(1)} fusion(f32[8,3,256,256]{3,2,1,0:T(8,128)} %param.12, f32[8,3,64,256]{3,2,1,0:T(8,128)} %bitcast.165, pred[8,3]{1,0:T(8,128)(4,1)S(1)} %copy.48), kind=kOutput, calls=%fused_computation.10 | convolution fusion | flops 1208352768 | bytes 8388632 | tf_op jit(solution)/shard_map/pcjt,cjts->pcs/dot_general | solution.py:19
  61.5 1.8 gather_fusion.2
  63.4 1.7 slice_multiply_fusion.12
  65.0 2.3 %slice_multiply_fusion.14 = f32[2,1,16,2048]{3,2,1,0:T(8,128)} fusion(f32[2,2,16,2048]{3,2,1,0:T(8,128)} %reshape_reshape.40, f32[]{:T(128)} %bitcast.23), kind=kLoop, calls=%fused_computation.82 | loop fusion | flops 65536 | bytes 524292 | tf_op jit(solution)/shard_map/mul | solution.py:37
  67.3 2.4 %slice_multiply_fusion.16 = f32[4,1,8,2048]{3,2,1,0:T(8,128)} fusion(f32[4,2,8,2048]{3,2,1,0:T(8,128)} %reshape_reshape.39, f32[]{:T(128)} %bitcast.19), kind=kLoop, calls=%fused_computation.84 | loop fusion | flops 65536 | bytes 524292 | tf_op jit(solution)/shard_map/mul | solution.py:37
  69.7 1.8 broadcast_select_fusion.11
  71.5 3.3 %collective-permute-start.5 = (f32[64,2048]{1,0:T(8,128)}, f32[64,2048]{1,0:T(8,128)}, u32[]{:S(2)}, u32[]{:S(2)}) collective-permute-start(f32[64,2048]{1,0:T(8,128)} %get-tuple-element.19), channel_id=1, source_target_pairs={{0,64},{2,66},{4,68},{6,70},{8,72},{10,74},{12,76},{14,78},{16,80}... | collective-permute-start | bytes 1572872 | tf_op jit(solution)/shard_map/ppermute | solution.py:12
  75.5 3.9 %collective-permute-start.3 = (f32[64,2048]{1,0:T(8,128)}, f32[64,2048]{1,0:T(8,128)}, u32[]{:S(2)}, u32[]{:S(2)}) collective-permute-start(f32[64,2048]{1,0:T(8,128)} %get-tuple-element.16), channel_id=1, source_target_pairs={{0,16},{2,18},{4,20},{6,22},{8,24},{10,26},{12,28},{14,30},{16,0},... | collective-permute-start | bytes 1572872 | tf_op jit(solution)/shard_map/ppermute | solution.py:12
  80.4 3.0 %collective-permute-start.1 = (f32[64,2048]{1,0:T(8,128)}, f32[64,2048]{1,0:T(8,128)}, u32[]{:S(2)}, u32[]{:S(2)}) collective-permute-start(f32[64,2048]{1,0:T(8,128)} %get-tuple-element.18), channel_id=1, source_target_pairs={{0,4},{2,6},{4,0},{6,2},{8,12},{10,14},{12,8},{14,10},{16,20},{18,... | collective-permute-start | bytes 1572872 | tf_op jit(solution)/shard_map/ppermute | solution.py:12
  85.2 6.2 %fusion.12 = f32[8,8,8,256]{3,2,1,0:T(8,128)S(1)} fusion(f32[8,3,256,256]{3,2,1,0:T(8,128)} %param.10, f32[8,3,64,256]{3,2,1,0:T(8,128)S(1)} %bitcast.162, pred[8,3]{1,0:T(8,128)(4,1)S(1)} %copy.44), kind=kOutput, calls=%fused_computation.18 | convolution fusion | flops 1208352768 | bytes 8388632 | tf_op jit(solution)/shard_map/pcjt,cjts->pcs/dot_general | solution.py:19
  92.9 1.6 slice_multiply_fusion.20
  94.7 2.1 %pad_maximum_fusion.1 = f32[16,2,2,2048]{3,2,1,0:T(2,128)} fusion(f32[16,1,2,2048]{3,2,1,0:T(2,128)S(1)} %slice_multiply_fusion.20, f32[16,1,2,2048]{3,2,1,0:T(2,128)} %slice_multiply_fusion.21), kind=kLoop, calls=%fused_computation.31 | loop fusion | flops 131072 | bytes 1048576 | tf_op jit(solution)/shard_map/stack | solution.py:36
  97.4 1.4 reshape.447
  100.9 2.1 %collective-permute-done.2 = f32[64,2048]{1,0:T(8,128)} collective-permute-done((f32[64,2048]{1,0:T(8,128)}, f32[64,2048]{1,0:T(8,128)}, u32[]{:S(2)}, u32[]{:S(2)}) %collective-permute-start.2) | collective-permute-done | bytes 524320 | tf_op jit(solution)/shard_map/ppermute | solution.py:12
  103.0 3.4 %fusion.45 = f32[64,2048]{1,0:T(8,128)} fusion(f32[64,2048]{1,0:T(8,128)S(1)} %copy-done.3, f32[64,2048]{1,0:T(8,128)S(1)} %bitcast.171, f32[1,2,32,2048]{3,2,1,0:T(8,128)S(1)} %pad_maximum_fusion.5, f32[2,2,16,2048]{3,2,1,0:T(8,128)S(1)} %pad_maximum_fusion.4, f32[4,2,8,2048]{3,2,1,0:T(8,128)S(1)} %pad_maximum_fusion.3, ...), kind=kLoop, calls=%fused_computation.65 | loop fusion | flops 2883584 | bytes 7864604 | tf_op jit(solution)/shard_map/add | solution.py:74
  106.4 1.2 reshape.463
  107.7 1.3 slice_multiply_fusion.1
  109.0 1.3 slice_multiply_fusion.3
  111.0 1.3 slice_multiply_fusion.7
  112.9 1.4 slice_multiply_fusion.9
  114.4 1.6 slice_multiply_fusion.11
  116.0 12.6 %all-gather.5.cloned.1.call-done = f32[64,4096]{1,0:T(8,128)} async-done(((f32[64,2048]{1,0:T(8,128)}), f32[64,4096]{1,0:T(8,128)}) %all-gather.5.cloned.1.call-update) | async-done | bytes 1048592 | tf_op jit(solution)/shard_map/all_gather | solution.py:61
  128.6 1.3 copy.84
  130.5 1.8 gather_fusion.5
  132.4 7.3 %fusion = f32[8,64,256,1]{2,1,3,0:T(8,128)S(1)} fusion(f32[8,3,256,256]{3,2,1,0:T(8,128)} %param.12, f32[8,3,64,256]{3,2,1,0:T(8,128)} %bitcast.164, pred[8,3]{1,0:T(8,128)(4,1)S(1)} %copy.48), kind=kOutput, calls=%fused_computation.6 | convolution fusion | flops 1208352768 | bytes 8388632 | tf_op jit(solution)/shard_map/pcjt,cjts->pcs/dot_general | solution.py:19
  144.8 7.7 %fusion.15 = f32[8,8,8,256]{3,2,1,0:T(8,128)} fusion(f32[8,3,256,256]{3,2,1,0:T(8,128)} %param.10, f32[8,3,64,256]{3,2,1,0:T(8,128)S(1)} %bitcast.163, pred[8,3]{1,0:T(8,128)(4,1)S(1)} %copy.44), kind=kOutput, calls=%fused_computation.19 | convolution fusion | flops 1208352768 | bytes 8388632 | tf_op jit(solution)/shard_map/pcjt,cjts->pcs/dot_general | solution.py:19
  153.3 1.3 slice_multiply_fusion.2
  154.6 1.4 slice_multiply_fusion.4
  156.1 2.0 %broadcast_select_fusion.10 = (f32[64,2048]{1,0:T(8,128)}, f32[64,2048]{1,0:T(8,128)}, f32[64,2048]{1,0:T(8,128)}, f32[64,2048]{1,0:T(8,128)}, f32[64,2048]{1,0:T(8,128)}, /*index=5*/f32[64,2048]{1,0:T(8,128)}) fusion(f32[64,2048]{1,0:T(8,128)S(1)} %copy-done.2, f32[64,2048]{1,0:T(8,128)S(1)} %bitcast.172, pred[]{:T(512)S(6)} %eq.116, pred[]{:T(512)S(6)} %eq.121, ...), kind=kLoop, calls=%fused_computation.102 | loop fusion | flops 786432 | bytes 4194310 | tf_op jit(solution)/shard_map/jit(_where)/select_n | solution.py:68
  158.1 3.0 %collective-permute-start.11 = (f32[64,2048]{1,0:T(8,128)}, f32[64,2048]{1,0:T(8,128)}, u32[]{:S(2)}, u32[]{:S(2)}) collective-permute-start(f32[64,2048]{1,0:T(8,128)} %get-tuple-element.9), channel_id=1, source_target_pairs={{0,64},{2,66},{4,68},{6,70},{8,72},{10,74},{12,76},{14,78},{16,80}... | collective-permute-start | bytes 1572872 | tf_op jit(solution)/shard_map/ppermute | solution.py:12
  161.7 3.2 %collective-permute-start.9 = (f32[64,2048]{1,0:T(8,128)}, f32[64,2048]{1,0:T(8,128)}, u32[]{:S(2)}, u32[]{:S(2)}) collective-permute-start(f32[64,2048]{1,0:T(8,128)} %get-tuple-element.11), channel_id=1, source_target_pairs={{0,16},{2,18},{4,20},{6,22},{8,24},{10,26},{12,28},{14,30},{16,0},... | collective-permute-start | bytes 1572872 | tf_op jit(solution)/shard_map/ppermute | solution.py:12
  165.5 2.7 %collective-permute-start.7 = (f32[64,2048]{1,0:T(8,128)}, f32[64,2048]{1,0:T(8,128)}, u32[]{:S(2)}, u32[]{:S(2)}) collective-permute-start(f32[64,2048]{1,0:T(8,128)} %get-tuple-element.13), channel_id=1, source_target_pairs={{0,4},{2,6},{4,0},{6,2},{8,12},{10,14},{12,8},{14,10},{16,20},{18,... | collective-permute-start | bytes 1572872 | tf_op jit(solution)/shard_map/ppermute | solution.py:12
  171.6 1.6 slice_multiply_fusion.8
  173.2 1.5 collective-permute-done.11
  174.7 2.1 %pad_maximum_fusion.7 = f32[16,2,2,2048]{3,2,1,0:T(2,128)} fusion(f32[16,1,2,2048]{3,2,1,0:T(2,128)S(1)} %slice_multiply_fusion.8, f32[16,1,2,2048]{3,2,1,0:T(2,128)} %slice_multiply_fusion.9), kind=kLoop, calls=%fused_computation.37 | loop fusion | flops 131072 | bytes 1048576 | tf_op jit(solution)/shard_map/stack | solution.py:36
  177.4 1.4 reshape.462
  181.0 3.9 %collective-permute-done.10 = f32[64,2048]{1,0:T(8,128)} collective-permute-done((f32[64,2048]{1,0:T(8,128)}, f32[64,2048]{1,0:T(8,128)}, u32[]{:S(2)}, u32[]{:S(2)}) %collective-permute-start.10) | collective-permute-done | bytes 524320 | tf_op jit(solution)/shard_map/ppermute | solution.py:12
  184.9 3.2 %collective-permute-done.8 = f32[64,2048]{1,0:T(8,128)} collective-permute-done((f32[64,2048]{1,0:T(8,128)}, f32[64,2048]{1,0:T(8,128)}, u32[]{:S(2)}, u32[]{:S(2)}) %collective-permute-start.8) | collective-permute-done | bytes 524320 | tf_op jit(solution)/shard_map/ppermute | solution.py:12
  188.1 3.4 %fusion.35 = f32[64,2048]{1,0:T(8,128)} fusion(f32[64,2048]{1,0:T(8,128)S(1)} %copy-done.2, f32[64,2048]{1,0:T(8,128)S(1)} %bitcast.170, f32[1,2,32,2048]{3,2,1,0:T(8,128)S(1)} %pad_maximum_fusion.11, f32[2,2,16,2048]{3,2,1,0:T(8,128)S(1)} %pad_maximum_fusion.10, f32[4,2,8,2048]{3,2,1,0:T(8,128)S(1)} %pad_maximum_fusion.9, ...), kind=kLoop, calls=%fused_computation.52 | loop fusion | flops 2883584 | bytes 7864604 | tf_op jit(solution)/shard_map/add | solution.py:74
  (119 shorter events, 36.1 us)
Async XLA Ops:
  6.5 4.7 %copy-start = (f32[8,2]{0,1:T(2,128)S(1)}, f32[8,2]{0,1:T(2,128)}, u32[]{:S(2)}) copy-start(f32[8,2]{0,1:T(2,128)} %param.15) | copy-start | bytes 196
  6.5 8.5 %copy-start.3 = (f32[64,2048]{1,0:T(8,128)S(1)}, f32[64,2048]{1,0:T(8,128)}, u32[]{:S(2)}) copy-start(f32[64,2048]{1,0:T(8,128)} %param.9) | copy-start | bytes 1572868
  6.5 4.7 %copy-start.18 = (s32[12]{0:T(128)S(1)}, s32[12]{0:T(128)}, u32[]{:S(2)}) copy-start(s32[12]{0:T(128)} %param.14) | copy-start | bytes 148
  6.5 40.2 %all-gather.3.cloned.1.call-start = ((), (), s32[]{:S(2)}) async-start(), calls=%async_computation | async-start | bytes 1572864 | tf_op jit(solution)/shard_map/all_gather | solution.py:61
  7.3 121.3 %all-gather.5.cloned.1.call-start = ((), (), s32[]{:S(2)}) async-start(), calls=%async_computation.1 | async-start | bytes 1572864 | tf_op jit(solution)/shard_map/all_gather | solution.py:61
  69.7 13.7 %copy-start.8 = (f32[8,2,4,2048]{3,2,1,0:T(4,128)S(1)}, f32[8,2,4,2048]{3,2,1,0:T(4,128)}, u32[]{:S(2)}) copy-start(f32[8,2,4,2048]{3,2,1,0:T(4,128)} %reshape_reshape.38) | copy-start | bytes 1572868
  69.7 15.2 %copy-start.12 = (f32[1,1,32,2048]{3,2,1,0:T(8,128)S(1)}, f32[1,1,32,2048]{3,2,1,0:T(8,128)}, u32[]{:S(2)}) copy-start(f32[1,1,32,2048]{3,2,1,0:T(8,128)} %slice_multiply_fusion.13) | copy-start | bytes 786436
  71.5 13.5 %copy-start.13 = (f32[8,1,4,2048]{3,2,1,0:T(4,128)S(1)}, f32[8,1,4,2048]{3,2,1,0:T(4,128)}, u32[]{:S(2)}) copy-start(f32[8,1,4,2048]{3,2,1,0:T(4,128)} %slice_multiply_fusion.19) | copy-start | bytes 786436
  71.5 23.0 %collective-permute-start.5 = (f32[64,2048]{1,0:T(8,128)}, f32[64,2048]{1,0:T(8,128)}, u32[]{:S(2)}, u32[]{:S(2)}) collective-permute-start(f32[64,2048]{1,0:T(8,128)} %get-tuple-element.19), channel_id=1, source_target_pairs={{0,64},{2,66},{4,68},{6,70},{8,72},{10,74},{12,76},{14,78},{16,80}... | collective-permute-start | bytes 1572872 | tf_op jit(solution)/shard_map/ppermute | solution.py:12
  74.8 26.1 %collective-permute-start.4 = (f32[64,2048]{1,0:T(8,128)}, f32[64,2048]{1,0:T(8,128)}, u32[]{:S(2)}, u32[]{:S(2)}) collective-permute-start(f32[64,2048]{1,0:T(8,128)} %get-tuple-element.15), channel_id=1, source_target_pairs={{0,32},{2,34},{4,36},{6,38},{8,40},{10,42},{12,44},{14,46},{16,48}... | collective-permute-start | bytes 1572872 | tf_op jit(solution)/shard_map/ppermute | solution.py:12
  75.5 25.4 %collective-permute-start.3 = (f32[64,2048]{1,0:T(8,128)}, f32[64,2048]{1,0:T(8,128)}, u32[]{:S(2)}, u32[]{:S(2)}) collective-permute-start(f32[64,2048]{1,0:T(8,128)} %get-tuple-element.16), channel_id=1, source_target_pairs={{0,16},{2,18},{4,20},{6,22},{8,24},{10,26},{12,28},{14,30},{16,0},... | collective-permute-start | bytes 1572872 | tf_op jit(solution)/shard_map/ppermute | solution.py:12
  79.4 23.6 %collective-permute-start.2 = (f32[64,2048]{1,0:T(8,128)}, f32[64,2048]{1,0:T(8,128)}, u32[]{:S(2)}, u32[]{:S(2)}) collective-permute-start(f32[64,2048]{1,0:T(8,128)} %get-tuple-element.17), channel_id=1, source_target_pairs={{0,8},{2,10},{4,12},{6,14},{8,0},{10,2},{12,4},{14,6},{16,24},{18,... | collective-permute-start | bytes 1572872 | tf_op jit(solution)/shard_map/ppermute | solution.py:12
  80.4 4.7 %copy-start.4 = (f32[24,64,256]{2,1,0:T(8,128)S(1)}, f32[24,64,256]{2,1,0:T(8,128)}, u32[]{:S(2)}) copy-start(f32[24,64,256]{2,1,0:T(8,128)} %gather_fusion.2) | copy-start | bytes 4718596
  80.4 22.6 %collective-permute-start.1 = (f32[64,2048]{1,0:T(8,128)}, f32[64,2048]{1,0:T(8,128)}, u32[]{:S(2)}, u32[]{:S(2)}) collective-permute-start(f32[64,2048]{1,0:T(8,128)} %get-tuple-element.18), channel_id=1, source_target_pairs={{0,4},{2,6},{4,0},{6,2},{8,12},{10,14},{12,8},{14,10},{16,20},{18,... | collective-permute-start | bytes 1572872 | tf_op jit(solution)/shard_map/ppermute | solution.py:12
  85.1 6.2 %copy-start.17 = (f32[32,1,1,2048]{3,1,0,2:T(1,128)S(1)}, f32[32,1,1,2048]{3,1,0,2:T(1,128)}, u32[]{:S(2)}) copy-start(f32[32,1,1,2048]{3,1,0,2:T(1,128)} %slice_multiply_fusion.23) | copy-start | bytes 786436
  94.6 8.4 %collective-permute-start = (f32[64,2048]{1,0:T(8,128)}, f32[64,2048]{1,0:T(8,128)}, u32[]{:S(2)}, u32[]{:S(2)}) collective-permute-start(f32[64,2048]{1,0:T(8,128)} %get-tuple-element.14), channel_id=1, source_target_pairs={{0,2},{2,0},{4,6},{6,4},{8,10},{10,8},{12,14},{14,12},{16,18},{18,... | collective-permute-start | bytes 1572872 | tf_op jit(solution)/shard_map/ppermute | solution.py:12
  106.4 1.3 copy-start.2
  144.8 7.7 %copy-start.11 = (f32[1,2,32,2048]{3,2,1,0:T(8,128)S(1)}, f32[1,2,32,2048]{3,2,1,0:T(8,128)}, u32[]{:S(2)}) copy-start(f32[1,2,32,2048]{3,2,1,0:T(8,128)} %reshape_reshape.47) | copy-start | bytes 1572868
  144.8 8.5 %copy-start.10 = (f32[2,2,16,2048]{3,2,1,0:T(8,128)S(1)}, f32[2,2,16,2048]{3,2,1,0:T(8,128)}, u32[]{:S(2)}) copy-start(f32[2,2,16,2048]{3,2,1,0:T(8,128)} %reshape_reshape.46) | copy-start | bytes 1572868
  144.8 9.8 %copy-start.9 = (f32[4,2,8,2048]{3,2,1,0:T(8,128)S(1)}, f32[4,2,8,2048]{3,2,1,0:T(8,128)}, u32[]{:S(2)}) copy-start(f32[4,2,8,2048]{3,2,1,0:T(8,128)} %reshape_reshape.45) | copy-start | bytes 1572868
  156.0 12.1 %copy-start.7 = (f32[8,2,4,2048]{3,2,1,0:T(4,128)S(1)}, f32[8,2,4,2048]{3,2,1,0:T(4,128)}, u32[]{:S(2)}) copy-start(f32[8,2,4,2048]{3,2,1,0:T(4,128)} %reshape_reshape.44) | copy-start | bytes 1572868
  156.0 12.8 %copy-start.6 = (f32[32,2,1,2048]{3,1,0,2:T(2,128)S(1)}, f32[32,2,1,2048]{3,1,0,2:T(2,128)}, u32[]{:S(2)}) copy-start(f32[32,2,1,2048]{3,1,0,2:T(2,128)} %reshape_reshape.42) | copy-start | bytes 1572868
  156.1 13.6 %copy-start.14 = (f32[1,1,32,2048]{3,2,1,0:T(8,128)S(1)}, f32[1,1,32,2048]{3,2,1,0:T(8,128)}, u32[]{:S(2)}) copy-start(f32[1,1,32,2048]{3,2,1,0:T(8,128)} %slice_multiply_fusion.1) | copy-start | bytes 786436
  158.1 11.7 %copy-start.15 = (f32[8,1,4,2048]{3,2,1,0:T(4,128)S(1)}, f32[8,1,4,2048]{3,2,1,0:T(4,128)}, u32[]{:S(2)}) copy-start(f32[8,1,4,2048]{3,2,1,0:T(4,128)} %slice_multiply_fusion.7) | copy-start | bytes 786436
  158.1 16.6 %collective-permute-start.11 = (f32[64,2048]{1,0:T(8,128)}, f32[64,2048]{1,0:T(8,128)}, u32[]{:S(2)}, u32[]{:S(2)}) collective-permute-start(f32[64,2048]{1,0:T(8,128)} %get-tuple-element.9), channel_id=1, source_target_pairs={{0,64},{2,66},{4,68},{6,70},{8,72},{10,74},{12,76},{14,78},{16,80}... | collective-permute-start | bytes 1572872 | tf_op jit(solution)/shard_map/ppermute | solution.py:12
  161.1 23.8 %collective-permute-start.10 = (f32[64,2048]{1,0:T(8,128)}, f32[64,2048]{1,0:T(8,128)}, u32[]{:S(2)}, u32[]{:S(2)}) collective-permute-start(f32[64,2048]{1,0:T(8,128)} %get-tuple-element.10), channel_id=1, source_target_pairs={{0,32},{2,34},{4,36},{6,38},{8,40},{10,42},{12,44},{14,46},{16,48}... | collective-permute-start | bytes 1572872 | tf_op jit(solution)/shard_map/ppermute | solution.py:12
  161.7 23.2 %collective-permute-start.9 = (f32[64,2048]{1,0:T(8,128)}, f32[64,2048]{1,0:T(8,128)}, u32[]{:S(2)}, u32[]{:S(2)}) collective-permute-start(f32[64,2048]{1,0:T(8,128)} %get-tuple-element.11), channel_id=1, source_target_pairs={{0,16},{2,18},{4,20},{6,22},{8,24},{10,26},{12,28},{14,30},{16,0},... | collective-permute-start | bytes 1572872 | tf_op jit(solution)/shard_map/ppermute | solution.py:12
  164.8 23.3 %collective-permute-start.8 = (f32[64,2048]{1,0:T(8,128)}, f32[64,2048]{1,0:T(8,128)}, u32[]{:S(2)}, u32[]{:S(2)}) collective-permute-start(f32[64,2048]{1,0:T(8,128)} %get-tuple-element.12), channel_id=1, source_target_pairs={{0,8},{2,10},{4,12},{6,14},{8,0},{10,2},{12,4},{14,6},{16,24},{18,... | collective-permute-start | bytes 1572872 | tf_op jit(solution)/shard_map/ppermute | solution.py:12
  165.5 4.4 %copy-start.16 = (f32[32,1,1,2048]{3,1,0,2:T(1,128)S(1)}, f32[32,1,1,2048]{3,1,0,2:T(1,128)}, u32[]{:S(2)}) copy-start(f32[32,1,1,2048]{3,1,0,2:T(1,128)} %slice_multiply_fusion.11) | copy-start | bytes 786436
  165.5 22.6 %collective-permute-start.7 = (f32[64,2048]{1,0:T(8,128)}, f32[64,2048]{1,0:T(8,128)}, u32[]{:S(2)}, u32[]{:S(2)}) collective-permute-start(f32[64,2048]{1,0:T(8,128)} %get-tuple-element.13), channel_id=1, source_target_pairs={{0,4},{2,6},{4,0},{6,2},{8,12},{10,14},{12,8},{14,10},{16,20},{18,... | collective-permute-start | bytes 1572872 | tf_op jit(solution)/shard_map/ppermute | solution.py:12
  170.4 6.4 %copy-start.5 = (f32[8,8,8,256]{3,2,1,0:T(8,128)S(1)}, f32[8,8,8,256]{3,2,1,0:T(8,128)}, u32[]{:S(2)}) copy-start(f32[8,8,8,256]{3,2,1,0:T(8,128)} %fusion.15) | copy-start | bytes 1572868
  174.7 13.4 %collective-permute-start.6 = (f32[64,2048]{1,0:T(8,128)}, f32[64,2048]{1,0:T(8,128)}, u32[]{:S(2)}, u32[]{:S(2)}) collective-permute-start(f32[64,2048]{1,0:T(8,128)} %get-tuple-element.8), channel_id=1, source_target_pairs={{0,2},{2,0},{4,6},{6,4},{8,10},{10,8},{12,14},{14,12},{16,18},{18,... | collective-permute-start | bytes 1572872 | tf_op jit(solution)/shard_map/ppermute | solution.py:12
  188.1 3.4 %copy-start.1 = (f32[8,2]{0,1:T(2,128)S(1)}, f32[8,2]{0,1:T(2,128)}, u32[]{:S(2)}) copy-start(f32[8,2]{0,1:T(2,128)} %param.15) | copy-start | bytes 196
Sparse Core Ops, SparseCore 0:
  9.0 26.2 all-gather.2
  106.6 21.9 all-gather.4
where the time goes:
time: 200 us; the launch traced here: 198 us
  other arithmetic  62.4 us (31%)
  local copies, waits for them, and re-layouts  31.7 us (16%)
  between operations  29.6 us (15%)
  matrix products  28.4 us (14%)
  waiting for transfers between devices  24.1 us (12%)
  starting transfers between devices  22.1 us (11%)
    dot_general x4, matrix products, apply_blocks(): jnp.einsum('pcjt,cjts->pcs', chosen, blocks, precision=lax.Precision.HIGH...  28.4 us
    ppermute x12, starting transfers between devices, from_partner(): return lax.ppermute(value, axis, pairs)  22.1 us
    mul x12, other arithmetic, bit_terms(): fail[first + bit] * lower[:, 0]  16 us
    mul x12, other arithmetic, bit_terms(): repair[first + bit] * upper[:, 1]  15.3 us
    all_gather x2, waiting for transfers between devices, local(): whole = lax.all_gather(current, 'queue', axis=1, tiled=True)  12.6 us
    another operation x12, local copies, waits for them, and re-layouts, bit_terms(): lower = killed.reshape(shape)  11 us
    ppermute x12, waiting for transfers between devices, from_partner(): return lax.ppermute(value, axis, pairs)  10.8 us
    another operation x12, other arithmetic, bit_terms(): jnp.stack((repair[first + bit] * upper[:, 1], fail[first + bit] * lower[:...  9.75 us
  transfers between devices with their start and end apart: 14, of which 5 were waited for; matrix products, arithmetic and copies ran while one was open for 31% of the time, Pallas kernels for 0%

commit v1 on v0

--- a/solution.py
+++ b/solution.py
@@ -58,7 +58,9 @@
         leaving = leaving + jnp.where(flag == 1, repair[low_count + bit], fail[low_count + bit])
     current = state
     for step in range(STEPS):
-        whole = lax.all_gather(current, "queue", axis=1, tiled=True)
+        whole = jnp.concatenate(
+            lax.all_to_all(jnp.stack([current] * lax.axis_size("queue")), "queue", 0, 0), axis=1
+        )
         queue_part = apply_blocks(whole, queue_blocks, queue_rows)
         killed = apply_blocks(whole, kill_blocks, kill_rows)
         rack_part = bit_terms(current, killed, fail, repair, 0, low_count)

time: 200 us -> 184 us (0.920)
  between operations: 29.6 us -> 16.5 us
  waiting for transfers between devices: 24.1 us -> 13.8 us
  local copies, waits for them, and re-layouts: 31.7 us -> 37.1 us
  starting transfers between devices: 22.1 us -> 25.2 us
    all_gather x2 -> x0, waiting for transfers between devices: 12.6 us -> none  [local(): whole = lax.all_gather(current, 'queue', axis=1, tiled=True)]
    another operation x0 -> x4, local copies, waits for them, and re-layouts: none -> 7.34 us  [apply_blocks(): pieces = whole.reshape(patterns, -1, blocks.shape[2])]
    all_to_all x0 -> x2, starting transfers between devices: none -> 7.16 us  [local(): lax.all_to_all(jnp.stack([current] * lax.axis_size('queue')), 'queue', 0, 0)]
    all_to_all x0 -> x2, waiting for transfers between devices: none -> 4.3 us  [local(): lax.all_to_all(jnp.stack([current] * lax.axis_size('queue')), 'queue', 0, 0)]
    ppermute x12, starting transfers between devices: 22.1 us -> 18 us  [from_partner(): return lax.ppermute(value, axis, pairs)]
    another operation x0 -> x2, other arithmetic: none -> 3.46 us  [local(): jnp.stack([current] * lax.axis_size('queue'))]
    reshape x6, local copies, waits for them, and re-layouts: 3.65 us -> 1.52 us  [bit_terms(): upper = current.reshape(shape)]
  transfers between devices with their start and end apart: 14 -> 14, of which waited for: 5 -> 4; matrix products, arithmetic and copies ran while one was open for 31% -> 31% of each run, Pallas kernels for 0% -> 0%
where the time goes in v1:
time: 184 us; the launch traced here: 182 us
  other arithmetic  61.3 us (33%)
  local copies, waits for them, and re-layouts  37.1 us (20%)
  matrix products  28.4 us (15%)
  starting transfers between devices  25.2 us (14%)
  between operations  16.5 us (9%)
  waiting for transfers between devices  13.8 us (8%)
    dot_general x4, matrix products, apply_blocks(): jnp.einsum('pcjt,cjts->pcs', chosen, blocks, precision=lax.Precision.HIGH...  28.4 us
    ppermute x12, starting transfers between devices, from_partner(): return lax.ppermute(value, axis, pairs)  18 us
    mul x12, other arithmetic, bit_terms(): repair[first + bit] * upper[:, 1]  15.6 us
    mul x12, other arithmetic, bit_terms(): fail[first + bit] * lower[:, 0]  14.9 us
    another operation x12, local copies, waits for them, and re-layouts, bit_terms(): lower = killed.reshape(shape)  10.3 us
    another operation x12, other arithmetic, bit_terms(): jnp.stack((repair[first + bit] * upper[:, 1], fail[first + bit] * lower[:...  9.64 us
    ppermute x12, waiting for transfers between devices, from_partner(): return lax.ppermute(value, axis, pairs)  9.53 us
    add x1, other arithmetic, local(): leaving + jnp.where(flag == 1, repair[low_count + bit], fail[low_count +...  7.44 us
  transfers between devices with their start and end apart: 14, of which 4 were waited for; matrix products, arithmetic and copies ran while one was open for 31% of the time, Pallas kernels for 0%

profile of v1, /device:TPU:0, one launch (start us, length us, event | category | flops | bytes accessed | tf_op | source)
XLA Modules:
  0.0 182.5 jit_solution(6956170318375877922)
XLA Ops:
  0.0 2.4 %pad_maximum_fusion = f32[2,64,2048]{2,1,0:T(8,128)} fusion(f32[1,64,2048]{2,1,0:T(8,128)} %bitcast.152), kind=kLoop, calls=%fused_computation.20 | loop fusion | flops 262144 | bytes 1572864 | tf_op jit(solution)/shard_map/stack | solution.py:62
  2.4 3.6 %all-to-all-start = ((f32[2,64,2048]{2,1,0:T(8,128)}), f32[2,64,2048]{2,1,0:T(8,128)S(1)}, u32[]{:S(2)}, u32[]{:S(2)}) async-start(f32[2,64,2048]{2,1,0:T(8,128)} %pad_maximum_fusion), calls=%async_computation | async-start | bytes 2097152 | tf_op jit(solution)/shard_map/all_to_all | solution.py:62
  26.2 1.3 slice_multiply_fusion.13
  27.6 1.4 slice_multiply_fusion.15
  29.6 1.3 slice_multiply_fusion.19
  30.9 1.6 slice_multiply_fusion.21
  33.1 7.4 %add_add_fusion = f32[64]{0:T(128)S(1)} fusion(f32[]{:T(128)S(6)} %select_n.398, f32[]{:T(128)S(6)} %select_n.397, f32[]{:T(128)S(6)} %select_n.396, f32[]{:T(128)S(6)} %select_n.395, f32[]{:T(128)S(6)} %select_n.394, f32[]{:T(128)S(6)} %select_n.393, f32[]{:T(128)} %bitcast.29, f32[]{:T(128)} %bitcast.27, f32[]{:T(128)} %bitcast.25, f32[]{:T(128)} %bitcast.23, ...), kind=kLoop, calls=%fused_computation.162 | loop fusion | flops 7296 | bytes 328 | tf_op jit(solution)/shard_map/add | solution.py:58
  40.6 1.6 slice_multiply_fusion.23
  42.9 1.8 %reshape_reshape.44 = f32[64,16,256]{2,1,0:T(8,128)} reshape(f32[64,2,2048]{2,1,0:T(2,128)S(1)} %copy.17) | data formatting | bytes 2097152 | tf_op jit(solution)/shard_map/reshape;reshape | solution.py:17
  44.8 1.8 %copy.19 = f32[64,16,256]{2,0,1:T(8,128)S(1)} copy(f32[64,16,256]{2,1,0:T(8,128)} %reshape_reshape.44) | data formatting | bytes 2097152 | tf_op jit(solution)/shard_map/reshape;reshape | solution.py:17
  46.6 1.8 %gather_fusion.3 = f32[24,64,256]{2,1,0:T(8,128)} fusion(f32[64,16,256]{2,0,1:T(8,128)S(1)} %copy.19, s32[1024]{0:T(1024)S(1)} %pad_clamp_fusion), kind=kCustom, calls=%fused_computation.1.clone | custom fusion | bytes 3145824 | tf_op jit(solution)/shard_map/jit(_take)/gather | solution.py:18
  48.4 7.3 %fusion.4 = f32[8,64,256,1]{2,1,3,0:T(8,128)S(1)} fusion(f32[8,3,256,256]{3,2,1,0:T(8,128)} %param.12, f32[8,3,64,256]{3,2,1,0:T(8,128)} %bitcast.159, pred[8,3]{1,0:T(8,128)(4,1)S(1)} %copy.21), kind=kOutput, calls=%fused_computation.10 | convolution fusion | flops 1208352768 | bytes 8388632 | tf_op jit(solution)/shard_map/pcjt,cjts->pcs/dot_general | solution.py:19
  60.1 1.8 %gather_fusion.2 = f32[24,64,256]{2,1,0:T(8,128)} fusion(f32[64,16,256]{2,0,1:T(8,128)S(1)} %copy.19, s32[1024]{0:T(1024)S(1)} %pad_clamp_fusion.1), kind=kCustom, calls=%fused_computation.clone | custom fusion | bytes 3145824 | tf_op jit(solution)/shard_map/jit(_take)/gather | solution.py:18
  61.9 1.5 slice_multiply_fusion.12
  63.4 2.3 %slice_multiply_fusion.14 = f32[2,1,16,2048]{3,2,1,0:T(8,128)} fusion(f32[2,2,16,2048]{3,2,1,0:T(8,128)} %reshape_reshape.49, f32[]{:T(128)} %bitcast.25), kind=kLoop, calls=%fused_computation.82 | loop fusion | flops 65536 | bytes 524292 | tf_op jit(solution)/shard_map/mul | solution.py:37
  65.7 2.3 %slice_multiply_fusion.16 = f32[4,1,8,2048]{3,2,1,0:T(8,128)} fusion(f32[4,2,8,2048]{3,2,1,0:T(8,128)} %reshape_reshape.48, f32[]{:T(128)} %bitcast.21), kind=kLoop, calls=%fused_computation.84 | loop fusion | flops 65536 | bytes 524292 | tf_op jit(solution)/shard_map/mul | solution.py:37
  68.1 1.8 broadcast_select_fusion.11
  69.9 3.3 %collective-permute-start.5 = (f32[64,2048]{1,0:T(8,128)}, f32[64,2048]{1,0:T(8,128)}, u32[]{:S(2)}, u32[]{:S(2)}) collective-permute-start(f32[64,2048]{1,0:T(8,128)} %get-tuple-element.19), channel_id=1, source_target_pairs={{0,64},{2,66},{4,68},{6,70},{8,72},{10,74},{12,76},{14,78},{16,80}... | collective-permute-start | bytes 1572872 | tf_op jit(solution)/shard_map/ppermute | solution.py:12
  73.8 3.9 %collective-permute-start.3 = (f32[64,2048]{1,0:T(8,128)}, f32[64,2048]{1,0:T(8,128)}, u32[]{:S(2)}, u32[]{:S(2)}) collective-permute-start(f32[64,2048]{1,0:T(8,128)} %get-tuple-element.16), channel_id=1, source_target_pairs={{0,16},{2,18},{4,20},{6,22},{8,24},{10,26},{12,28},{14,30},{16,0},... | collective-permute-start | bytes 1572872 | tf_op jit(solution)/shard_map/ppermute | solution.py:12
  78.7 3.0 %collective-permute-start.1 = (f32[64,2048]{1,0:T(8,128)}, f32[64,2048]{1,0:T(8,128)}, u32[]{:S(2)}, u32[]{:S(2)}) collective-permute-start(f32[64,2048]{1,0:T(8,128)} %get-tuple-element.18), channel_id=1, source_target_pairs={{0,4},{2,6},{4,0},{6,2},{8,12},{10,14},{12,8},{14,10},{16,20},{18,... | collective-permute-start | bytes 1572872 | tf_op jit(solution)/shard_map/ppermute | solution.py:12
  83.5 6.2 %fusion.12 = f32[8,8,8,256]{3,2,1,0:T(8,128)S(1)} fusion(f32[8,3,256,256]{3,2,1,0:T(8,128)} %param.10, f32[8,3,64,256]{3,2,1,0:T(8,128)S(1)} %bitcast.156, pred[8,3]{1,0:T(8,128)(4,1)S(1)} %copy.16), kind=kOutput, calls=%fused_computation.18 | convolution fusion | flops 1208352768 | bytes 8388632 | tf_op jit(solution)/shard_map/pcjt,cjts->pcs/dot_general | solution.py:19
  89.7 1.3 pad_maximum_fusion.2
  92.2 2.2 %pad_maximum_fusion.3 = f32[16,2,2,2048]{3,2,1,0:T(2,128)} fusion(f32[16,1,2,2048]{3,2,1,0:T(2,128)S(1)} %slice_multiply_fusion.20, f32[16,1,2,2048]{3,2,1,0:T(2,128)} %slice_multiply_fusion.21), kind=kLoop, calls=%fused_computation.31 | loop fusion | flops 131072 | bytes 1048576 | tf_op jit(solution)/shard_map/stack | solution.py:36
  95.0 2.3 %reshape.445 = f32[64,2048]{1,0:T(8,128)} reshape(f32[16,2,2,2048]{3,2,1,0:T(2,128)} %pad_maximum_fusion.3) | data formatting | bytes 1048576 | tf_op jit(solution)/shard_map/reshape | solution.py:39
  98.5 2.8 %collective-permute-done.2 = f32[64,2048]{1,0:T(8,128)} collective-permute-done((f32[64,2048]{1,0:T(8,128)}, f32[64,2048]{1,0:T(8,128)}, u32[]{:S(2)}, u32[]{:S(2)}) %collective-permute-start.2) | collective-permute-done | bytes 524320 | tf_op jit(solution)/shard_map/ppermute | solution.py:12
  101.4 2.5 %fusion.45 = f32[64,2048]{1,0:T(8,128)S(1)} fusion(f32[64,2048]{1,0:T(8,128)S(1)} %copy-done.2, f32[64,2048]{1,0:T(8,128)S(1)} %bitcast.167, f32[1,2,32,2048]{3,2,1,0:T(8,128)S(1)} %pad_maximum_fusion.7, f32[2,2,16,2048]{3,2,1,0:T(8,128)S(1)} %pad_maximum_fusion.6, f32[4,2,8,2048]{3,2,1,0:T(8,128)S(1)} %pad_maximum_fusion.5, ...), kind=kLoop, calls=%fused_computation.65 | loop fusion | flops 2883584 | bytes 7864604 | tf_op jit(solution)/shard_map/add | solution.py:76
  105.5 3.6 %all-to-all-start.1 = ((f32[2,64,2048]{2,1,0:T(8,128)}), f32[2,64,2048]{2,1,0:T(8,128)S(1)}, u32[]{:S(2)}, u32[]{:S(2)}) async-start(f32[2,64,2048]{2,1,0:T(8,128)} %pad_maximum_fusion.1), calls=%async_computation.1 | async-start | bytes 2097152 | tf_op jit(solution)/shard_map/all_to_all | solution.py:62
  110.4 1.4 slice_multiply_fusion.3
  112.4 1.4 slice_multiply_fusion.7
  113.8 1.5 slice_multiply_fusion.9
  115.6 1.6 slice_multiply_fusion.11
  117.2 4.3 %all-to-all-done.1 = f32[2,64,2048]{2,1,0:T(8,128)S(1)} async-done(((f32[2,64,2048]{2,1,0:T(8,128)}), f32[2,64,2048]{2,1,0:T(8,128)S(1)}, u32[]{:S(2)}, u32[]{:S(2)}) %all-to-all-start.1) | async-done | bytes 1048608 | tf_op jit(solution)/shard_map/all_to_all | solution.py:62
  122.3 1.8 %reshape_reshape.51 = f32[64,16,256]{2,1,0:T(8,128)} reshape(f32[64,2,2048]{2,1,0:T(2,128)S(1)} %copy.32) | data formatting | bytes 2097152 | tf_op jit(solution)/shard_map/reshape;reshape | solution.py:17
  124.1 1.8 %copy.34 = f32[64,16,256]{2,0,1:T(8,128)S(1)} copy(f32[64,16,256]{2,1,0:T(8,128)} %reshape_reshape.51) | data formatting | bytes 2097152 | tf_op jit(solution)/shard_map/reshape;reshape | solution.py:17
  125.9 1.8 %gather_fusion.4 = f32[24,64,256]{2,1,0:T(8,128)} fusion(f32[64,16,256]{2,0,1:T(8,128)S(1)} %copy.34, s32[1024]{0:T(1024)S(1)} %pad_clamp_fusion.1), kind=kCustom, calls=%fused_computation.2.clone | custom fusion | bytes 3145824 | tf_op jit(solution)/shard_map/jit(_take)/gather | solution.py:18
  127.8 1.8 gather_fusion.5
  129.6 7.3 %fusion = f32[8,64,256,1]{2,1,3,0:T(8,128)S(1)} fusion(f32[8,3,256,256]{3,2,1,0:T(8,128)} %param.12, f32[8,3,64,256]{3,2,1,0:T(8,128)} %bitcast.158, pred[8,3]{1,0:T(8,128)(4,1)S(1)} %copy.21), kind=kOutput, calls=%fused_computation.6 | convolution fusion | flops 1208352768 | bytes 8388632 | tf_op jit(solution)/shard_map/pcjt,cjts->pcs/dot_general | solution.py:19
  142.0 7.7 %fusion.15 = f32[8,8,8,256]{3,2,1,0:T(8,128)} fusion(f32[8,3,256,256]{3,2,1,0:T(8,128)} %param.10, f32[8,3,64,256]{3,2,1,0:T(8,128)S(1)} %bitcast.157, pred[8,3]{1,0:T(8,128)(4,1)S(1)} %copy.16), kind=kOutput, calls=%fused_computation.19 | convolution fusion | flops 1208352768 | bytes 8388632 | tf_op jit(solution)/shard_map/pcjt,cjts->pcs/dot_general | solution.py:19
  150.3 1.4 slice_multiply_fusion.2
  151.7 1.4 slice_multiply_fusion.4
  153.1 1.9 %broadcast_select_fusion.10 = (f32[64,2048]{1,0:T(8,128)}, f32[64,2048]{1,0:T(8,128)}, f32[64,2048]{1,0:T(8,128)}, f32[64,2048]{1,0:T(8,128)}, f32[64,2048]{1,0:T(8,128)}, /*index=5*/f32[64,2048]{1,0:T(8,128)}) fusion(f32[64,2048]{1,0:T(8,128)S(1)} %fusion.45, f32[64,2048]{1,0:T(8,128)S(1)} %bitcast.168, pred[]{:T(512)S(6)} %eq.116, pred[]{:T(512)S(6)} %eq.121, ...), kind=kLoop, calls=%fused_computation.102 | loop fusion | flops 786432 | bytes 4194310 | tf_op jit(solution)/shard_map/jit(_where)/select_n | solution.py:70
  155.0 1.8 %collective-permute-start.11 = (f32[64,2048]{1,0:T(8,128)}, f32[64,2048]{1,0:T(8,128)}, u32[]{:S(2)}, u32[]{:S(2)}) collective-permute-start(f32[64,2048]{1,0:T(8,128)} %get-tuple-element.9), channel_id=1, source_target_pairs={{0,64},{2,66},{4,68},{6,70},{8,72},{10,74},{12,76},{14,78},{16,80}... | collective-permute-start | bytes 1572872 | tf_op jit(solution)/shard_map/ppermute | solution.py:12
  158.1 3.0 %collective-permute-start.7 = (f32[64,2048]{1,0:T(8,128)}, f32[64,2048]{1,0:T(8,128)}, u32[]{:S(2)}, u32[]{:S(2)}) collective-permute-start(f32[64,2048]{1,0:T(8,128)} %get-tuple-element.13), channel_id=1, source_target_pairs={{0,4},{2,6},{4,0},{6,2},{8,12},{10,14},{12,8},{14,10},{16,20},{18,... | collective-permute-start | bytes 1572872 | tf_op jit(solution)/shard_map/ppermute | solution.py:12
  164.5 1.7 slice_multiply_fusion.8
  166.2 5.5 %collective-permute-done.11 = f32[64,2048]{1,0:T(8,128)} collective-permute-done((f32[64,2048]{1,0:T(8,128)}, f32[64,2048]{1,0:T(8,128)}, u32[]{:S(2)}, u32[]{:S(2)}) %collective-permute-start.11) | collective-permute-done | bytes 524320 | tf_op jit(solution)/shard_map/ppermute | solution.py:12
  171.7 2.1 %pad_maximum_fusion.9 = f32[16,2,2,2048]{3,2,1,0:T(2,128)} fusion(f32[16,1,2,2048]{3,2,1,0:T(2,128)S(1)} %slice_multiply_fusion.8, f32[16,1,2,2048]{3,2,1,0:T(2,128)} %slice_multiply_fusion.9), kind=kLoop, calls=%fused_computation.37 | loop fusion | flops 131072 | bytes 1048576 | tf_op jit(solution)/shard_map/stack | solution.py:36
  174.4 1.4 reshape.460
  179.1 3.4 %fusion.35 = f32[64,2048]{1,0:T(8,128)} fusion(f32[64,2048]{1,0:T(8,128)S(1)} %fusion.45, f32[64,2048]{1,0:T(8,128)S(1)} %bitcast.166, f32[1,2,32,2048]{3,2,1,0:T(8,128)S(1)} %pad_maximum_fusion.13, f32[2,2,16,2048]{3,2,1,0:T(8,128)S(1)} %pad_maximum_fusion.12, f32[4,2,8,2048]{3,2,1,0:T(8,128)S(1)} %pad_maximum_fusion.11, ...), kind=kLoop, calls=%fused_computation.52 | loop fusion | flops 2883584 | bytes 7864604 | tf_op jit(solution)/shard_map/add | solution.py:76
  (133 shorter events, 35.8 us)
Async XLA Ops:
  0.0 7.0 %copy-start = (f32[8,2]{0,1:T(2,128)S(1)}, f32[8,2]{0,1:T(2,128)}, u32[]{:S(2)}) copy-start(f32[8,2]{0,1:T(2,128)} %param.15) | copy-start | bytes 196
  0.0 6.0 %copy-start.21 = (s32[8,3]{0,1:T(4,128)S(1)}, s32[8,3]{0,1:T(4,128)}, u32[]{:S(2)}) copy-start(s32[8,3]{0,1:T(4,128)} %param.11) | copy-start | bytes 292
  0.0 6.0 %copy-start.22 = (s32[8,3]{0,1:T(4,128)S(1)}, s32[8,3]{0,1:T(4,128)}, u32[]{:S(2)}) copy-start(s32[8,3]{0,1:T(4,128)} %param.13) | copy-start | bytes 292
  0.0 6.1 %copy-start.2 = (f32[64,2048]{1,0:T(8,128)S(1)}, f32[64,2048]{1,0:T(8,128)}, u32[]{:S(2)}) copy-start(f32[64,2048]{1,0:T(8,128)} %param.9) | copy-start | bytes 1572868
  2.4 39.8 %all-to-all-start = ((f32[2,64,2048]{2,1,0:T(8,128)}), f32[2,64,2048]{2,1,0:T(8,128)S(1)}, u32[]{:S(2)}, u32[]{:S(2)}) async-start(f32[2,64,2048]{2,1,0:T(8,128)} %pad_maximum_fusion), calls=%async_computation | async-start | bytes 2097152 | tf_op jit(solution)/shard_map/all_to_all | solution.py:62
  6.2 0.8 copy-start.23
  68.1 13.7 %copy-start.10 = (f32[8,2,4,2048]{3,2,1,0:T(4,128)S(1)}, f32[8,2,4,2048]{3,2,1,0:T(4,128)}, u32[]{:S(2)}) copy-start(f32[8,2,4,2048]{3,2,1,0:T(4,128)} %reshape_reshape.47) | copy-start | bytes 1572868
  68.1 15.2 %copy-start.17 = (f32[1,1,32,2048]{3,2,1,0:T(8,128)S(1)}, f32[1,1,32,2048]{3,2,1,0:T(8,128)}, u32[]{:S(2)}) copy-start(f32[1,1,32,2048]{3,2,1,0:T(8,128)} %slice_multiply_fusion.13) | copy-start | bytes 786436
  69.9 13.5 %copy-start.18 = (f32[8,1,4,2048]{3,2,1,0:T(4,128)S(1)}, f32[8,1,4,2048]{3,2,1,0:T(4,128)}, u32[]{:S(2)}) copy-start(f32[8,1,4,2048]{3,2,1,0:T(4,128)} %slice_multiply_fusion.19) | copy-start | bytes 786436
  69.9 22.3 %collective-permute-start.5 = (f32[64,2048]{1,0:T(8,128)}, f32[64,2048]{1,0:T(8,128)}, u32[]{:S(2)}, u32[]{:S(2)}) collective-permute-start(f32[64,2048]{1,0:T(8,128)} %get-tuple-element.19), channel_id=1, source_target_pairs={{0,64},{2,66},{4,68},{6,70},{8,72},{10,74},{12,76},{14,78},{16,80}... | collective-permute-start | bytes 1572872 | tf_op jit(solution)/shard_map/ppermute | solution.py:12
  73.2 25.3 %collective-permute-start.4 = (f32[64,2048]{1,0:T(8,128)}, f32[64,2048]{1,0:T(8,128)}, u32[]{:S(2)}, u32[]{:S(2)}) collective-permute-start(f32[64,2048]{1,0:T(8,128)} %get-tuple-element.15), channel_id=1, source_target_pairs={{0,32},{2,34},{4,36},{6,38},{8,40},{10,42},{12,44},{14,46},{16,48}... | collective-permute-start | bytes 1572872 | tf_op jit(solution)/shard_map/ppermute | solution.py:12
  73.8 24.7 %collective-permute-start.3 = (f32[64,2048]{1,0:T(8,128)}, f32[64,2048]{1,0:T(8,128)}, u32[]{:S(2)}, u32[]{:S(2)}) collective-permute-start(f32[64,2048]{1,0:T(8,128)} %get-tuple-element.16), channel_id=1, source_target_pairs={{0,16},{2,18},{4,20},{6,22},{8,24},{10,26},{12,28},{14,30},{16,0},... | collective-permute-start | bytes 1572872 | tf_op jit(solution)/shard_map/ppermute | solution.py:12
  77.7 23.7 %collective-permute-start.2 = (f32[64,2048]{1,0:T(8,128)}, f32[64,2048]{1,0:T(8,128)}, u32[]{:S(2)}, u32[]{:S(2)}) collective-permute-start(f32[64,2048]{1,0:T(8,128)} %get-tuple-element.17), channel_id=1, source_target_pairs={{0,8},{2,10},{4,12},{6,14},{8,0},{10,2},{12,4},{14,6},{16,24},{18,... | collective-permute-start | bytes 1572872 | tf_op jit(solution)/shard_map/ppermute | solution.py:12
  78.7 4.7 %copy-start.3 = (f32[24,64,256]{2,1,0:T(8,128)S(1)}, f32[24,64,256]{2,1,0:T(8,128)}, u32[]{:S(2)}) copy-start(f32[24,64,256]{2,1,0:T(8,128)} %gather_fusion.2) | copy-start | bytes 4718596
  78.7 22.6 %collective-permute-start.1 = (f32[64,2048]{1,0:T(8,128)}, f32[64,2048]{1,0:T(8,128)}, u32[]{:S(2)}, u32[]{:S(2)}) collective-permute-start(f32[64,2048]{1,0:T(8,128)} %get-tuple-element.18), channel_id=1, source_target_pairs={{0,4},{2,6},{4,0},{6,2},{8,12},{10,14},{12,8},{14,10},{16,20},{18,... | collective-permute-start | bytes 1572872 | tf_op jit(solution)/shard_map/ppermute | solution.py:12
  83.5 6.2 %copy-start.20 = (f32[32,1,1,2048]{3,1,0,2:T(1,128)S(1)}, f32[32,1,1,2048]{3,1,0,2:T(1,128)}, u32[]{:S(2)}) copy-start(f32[32,1,1,2048]{3,1,0,2:T(1,128)} %slice_multiply_fusion.23) | copy-start | bytes 786436
  92.1 2.5 %copy-start.7 = (f32[32,2,1,2048]{3,1,0,2:T(2,128)S(1)}, f32[32,2,1,2048]{3,1,0,2:T(2,128)}, u32[]{:S(2)}) copy-start(f32[32,2,1,2048]{3,1,0,2:T(2,128)} %pad_maximum_fusion.2) | copy-start | bytes 1572868
  92.2 9.2 %collective-permute-start = (f32[64,2048]{1,0:T(8,128)}, f32[64,2048]{1,0:T(8,128)}, u32[]{:S(2)}, u32[]{:S(2)}) collective-permute-start(f32[64,2048]{1,0:T(8,128)} %get-tuple-element.14), channel_id=1, source_target_pairs={{0,2},{2,0},{4,6},{6,4},{8,10},{10,8},{12,14},{14,12},{16,18},{18,... | collective-permute-start | bytes 1572872 | tf_op jit(solution)/shard_map/ppermute | solution.py:12
  95.0 3.4 %copy-start.19 = (f32[4,1,8,2048]{3,2,1,0:T(8,128)S(1)}, f32[4,1,8,2048]{3,2,1,0:T(8,128)}, u32[]{:S(2)}) copy-start(f32[4,1,8,2048]{3,2,1,0:T(8,128)} %slice_multiply_fusion.16) | copy-start | bytes 786436
  97.3 4.1 %copy-start.6 = (f32[64,2048]{1,0:T(8,128)S(1)}, f32[64,2048]{1,0:T(8,128)}, u32[]{:S(2)}) copy-start(f32[64,2048]{1,0:T(8,128)} %reshape.445) | copy-start | bytes 1572868
  105.5 16.0 %all-to-all-start.1 = ((f32[2,64,2048]{2,1,0:T(8,128)}), f32[2,64,2048]{2,1,0:T(8,128)S(1)}, u32[]{:S(2)}, u32[]{:S(2)}) async-start(f32[2,64,2048]{2,1,0:T(8,128)} %pad_maximum_fusion.1), calls=%async_computation.1 | async-start | bytes 2097152 | tf_op jit(solution)/shard_map/all_to_all | solution.py:62
  139.0 3.1 %copy-start.4 = (f32[24,64,256]{2,1,0:T(8,128)S(1)}, f32[24,64,256]{2,1,0:T(8,128)}, u32[]{:S(2)}) copy-start(f32[24,64,256]{2,1,0:T(8,128)} %gather_fusion.4) | copy-start | bytes 4718596
  142.0 7.7 %copy-start.13 = (f32[1,2,32,2048]{3,2,1,0:T(8,128)S(1)}, f32[1,2,32,2048]{3,2,1,0:T(8,128)}, u32[]{:S(2)}) copy-start(f32[1,2,32,2048]{3,2,1,0:T(8,128)} %reshape_reshape.57) | copy-start | bytes 1572868
  142.0 8.3 %copy-start.12 = (f32[2,2,16,2048]{3,2,1,0:T(8,128)S(1)}, f32[2,2,16,2048]{3,2,1,0:T(8,128)}, u32[]{:S(2)}) copy-start(f32[2,2,16,2048]{3,2,1,0:T(8,128)} %reshape_reshape.56) | copy-start | bytes 1572868
  142.0 9.7 %copy-start.11 = (f32[4,2,8,2048]{3,2,1,0:T(8,128)S(1)}, f32[4,2,8,2048]{3,2,1,0:T(8,128)}, u32[]{:S(2)}) copy-start(f32[4,2,8,2048]{3,2,1,0:T(8,128)} %reshape_reshape.55) | copy-start | bytes 1572868
  153.1 8.0 %copy-start.9 = (f32[8,2,4,2048]{3,2,1,0:T(4,128)S(1)}, f32[8,2,4,2048]{3,2,1,0:T(4,128)}, u32[]{:S(2)}) copy-start(f32[8,2,4,2048]{3,2,1,0:T(4,128)} %reshape_reshape.54) | copy-start | bytes 1572868
  153.1 8.7 %copy-start.8 = (f32[32,2,1,2048]{3,1,0,2:T(2,128)S(1)}, f32[32,2,1,2048]{3,1,0,2:T(2,128)}, u32[]{:S(2)}) copy-start(f32[32,2,1,2048]{3,1,0,2:T(2,128)} %reshape_reshape.52) | copy-start | bytes 1572868
  153.1 9.5 %copy-start.14 = (f32[1,1,32,2048]{3,2,1,0:T(8,128)S(1)}, f32[1,1,32,2048]{3,2,1,0:T(8,128)}, u32[]{:S(2)}) copy-start(f32[1,1,32,2048]{3,2,1,0:T(8,128)} %slice_multiply_fusion.1) | copy-start | bytes 786436
  155.0 7.6 %copy-start.15 = (f32[8,1,4,2048]{3,2,1,0:T(4,128)S(1)}, f32[8,1,4,2048]{3,2,1,0:T(4,128)}, u32[]{:S(2)}) copy-start(f32[8,1,4,2048]{3,2,1,0:T(4,128)} %slice_multiply_fusion.7) | copy-start | bytes 786436
  155.0 16.7 %collective-permute-start.11 = (f32[64,2048]{1,0:T(8,128)}, f32[64,2048]{1,0:T(8,128)}, u32[]{:S(2)}, u32[]{:S(2)}) collective-permute-start(f32[64,2048]{1,0:T(8,128)} %get-tuple-element.9), channel_id=1, source_target_pairs={{0,64},{2,66},{4,68},{6,70},{8,72},{10,74},{12,76},{14,78},{16,80}... | collective-permute-start | bytes 1572872 | tf_op jit(solution)/shard_map/ppermute | solution.py:12
  156.9 21.0 %collective-permute-start.10 = (f32[64,2048]{1,0:T(8,128)}, f32[64,2048]{1,0:T(8,128)}, u32[]{:S(2)}, u32[]{:S(2)}) collective-permute-start(f32[64,2048]{1,0:T(8,128)} %get-tuple-element.10), channel_id=1, source_target_pairs={{0,32},{2,34},{4,36},{6,38},{8,40},{10,42},{12,44},{14,46},{16,48}... | collective-permute-start | bytes 1572872 | tf_op jit(solution)/shard_map/ppermute | solution.py:12
  156.9 21.0 %collective-permute-start.9 = (f32[64,2048]{1,0:T(8,128)}, f32[64,2048]{1,0:T(8,128)}, u32[]{:S(2)}, u32[]{:S(2)}) collective-permute-start(f32[64,2048]{1,0:T(8,128)} %get-tuple-element.11), channel_id=1, source_target_pairs={{0,16},{2,18},{4,20},{6,22},{8,24},{10,26},{12,28},{14,30},{16,0},... | collective-permute-start | bytes 1572872 | tf_op jit(solution)/shard_map/ppermute | solution.py:12
  158.0 21.0 %collective-permute-start.8 = (f32[64,2048]{1,0:T(8,128)}, f32[64,2048]{1,0:T(8,128)}, u32[]{:S(2)}, u32[]{:S(2)}) collective-permute-start(f32[64,2048]{1,0:T(8,128)} %get-tuple-element.12), channel_id=1, source_target_pairs={{0,8},{2,10},{4,12},{6,14},{8,0},{10,2},{12,4},{14,6},{16,24},{18,... | collective-permute-start | bytes 1572872 | tf_op jit(solution)/shard_map/ppermute | solution.py:12
  158.1 4.8 %copy-start.16 = (f32[32,1,1,2048]{3,1,0,2:T(1,128)S(1)}, f32[32,1,1,2048]{3,1,0,2:T(1,128)}, u32[]{:S(2)}) copy-start(f32[32,1,1,2048]{3,1,0,2:T(1,128)} %slice_multiply_fusion.11) | copy-start | bytes 786436
  158.1 21.0 %collective-permute-start.7 = (f32[64,2048]{1,0:T(8,128)}, f32[64,2048]{1,0:T(8,128)}, u32[]{:S(2)}, u32[]{:S(2)}) collective-permute-start(f32[64,2048]{1,0:T(8,128)} %get-tuple-element.13), channel_id=1, source_target_pairs={{0,4},{2,6},{4,0},{6,2},{8,12},{10,14},{12,8},{14,10},{16,20},{18,... | collective-permute-start | bytes 1572872 | tf_op jit(solution)/shard_map/ppermute | solution.py:12
  163.3 10.5 %copy-start.5 = (f32[8,8,8,256]{3,2,1,0:T(8,128)S(1)}, f32[8,8,8,256]{3,2,1,0:T(8,128)}, u32[]{:S(2)}) copy-start(f32[8,8,8,256]{3,2,1,0:T(8,128)} %fusion.15) | copy-start | bytes 1572868
  171.7 7.4 %collective-permute-start.6 = (f32[64,2048]{1,0:T(8,128)}, f32[64,2048]{1,0:T(8,128)}, u32[]{:S(2)}, u32[]{:S(2)}) collective-permute-start(f32[64,2048]{1,0:T(8,128)} %get-tuple-element.8), channel_id=1, source_target_pairs={{0,2},{2,0},{4,6},{6,4},{8,10},{10,8},{12,14},{14,12},{16,18},{18,... | collective-permute-start | bytes 1572872 | tf_op jit(solution)/shard_map/ppermute | solution.py:12
  179.1 3.4 %copy-start.1 = (f32[8,2]{0,1:T(2,128)S(1)}, f32[8,2]{0,1:T(2,128)}, u32[]{:S(2)}) copy-start(f32[8,2]{0,1:T(2,128)} %param.15) | copy-start | bytes 196
